TPU v7x, 256 devices: a whole 4x4x8 slice. The times are simulated.
256 devices in a mesh: pipe: 4 (over x), seq: 64 (over y, z, core).
Axes of the slice: x: 4, y: 4, z: 8, core: 2. Of those that a mesh axis runs over, the one named last changes fastest.
Arguments:
- acts: bfloat16 [4, 16384, 1024], P('pipe', 'seq'), may hold values from -6 to 6
- cotan: bfloat16 [4, 16384, 1024], P('pipe', 'seq'), may hold values from -6 to 6
- proj_in: bfloat16 [4, 1024, 2048], P('pipe'), may hold values from -0.1875 to 0.1875
- proj_out: bfloat16 [4, 1024, 1024], P('pipe'), may hold values from -0.1875 to 0.1875
- block_mix: bfloat16 [4, 16384, 256], P('pipe', 'seq'), may hold values from -0.375 to 0.375
- twiddle: float32 [4, 6, 2, 2, 1024], P('pipe'), may hold values from -2.5 to 2.5
Outputs:
- mixed: bfloat16 [4, 16384, 1024], P('pipe', 'seq')
- grad_prev: bfloat16 [4, 16384, 1024], P('pipe', 'seq')
- grad_in_proj: float32 [4, 1024, 2048], P('pipe', 'seq')
- grad_out_proj: float32 [4, 1024, 1024], P('pipe', 'seq')
- grad_block_mix: float32 [4, 16384, 256], P('pipe', 'seq')
- grad_twiddle: float32 [4, 6, 2, 2, 1024], P('pipe')
All inputs are finite; a program needn't handle non-finite values.
Results may differ from a plain program's by a relative error of at most 0.014.
Values may be sent and summed in bfloat16 or wider, within the bound.
A program may use at most 128 MiB of HBM per device.

v0:
```python
import jax
import jax.numpy as jnp
from jax import lax
from jax.sharding import PartitionSpec as P


def swapped(block, axis, apart):
    count = lax.axis_size(axis)
    route = []
    for low in range(count):
        high = low | 1 << apart
        if high != low and high < count:
            route += [(low, high), (high, low)]
    return lax.ppermute(block, axis, route)


def from_behind(value, axis, steps):
    count = lax.axis_size(axis)
    first, last = (max(0, -steps), min(count, count - steps))
    return lax.ppermute(value, axis, [(source, source + steps) for source in range(first, last)])


def on_device(acts, cotan, proj_in, proj_out, block_mix, twiddle):
    inputs = acts[0]
    grad_out = cotan[0]
    w_in = proj_in[0]
    w_out = proj_out[0]
    square_mix = block_mix[0]
    twiddle_w = twiddle[0]
    row_count, feature_count = inputs.shape
    seq_count = lax.axis_size("seq")
    segment_total = seq_count.bit_length() - 1
    position = lax.axis_index("seq")
    projected = jnp.dot(inputs, w_in, preferred_element_type=jnp.float32)
    value = projected[:, :feature_count].astype(jnp.bfloat16)
    gate = projected[:, feature_count:].astype(jnp.bfloat16)
    first_segment = jnp.dot(square_mix, value, preferred_element_type=jnp.float32).astype(
        jnp.bfloat16
    )
    partials = [None] * segment_total
    stored = []
    current = first_segment
    for segment_bit in range(segment_total):
        partner = swapped(current, "seq", segment_bit)
        upper_half = position >> segment_bit & 1
        segment_coef = jnp.where(
            upper_half == 0, twiddle_w[segment_bit, 0], twiddle_w[segment_bit, 1]
        )
        stored.append((current, partner))
        current = (
            segment_coef[0] * current.astype(jnp.float32)
            + segment_coef[1] * partner.astype(jnp.float32)
        ).astype(jnp.bfloat16)
    hidden = (current.astype(jnp.float32) * gate.astype(jnp.float32)).astype(jnp.bfloat16)
    mixed_out = jnp.dot(hidden, w_out, preferred_element_type=jnp.float32).astype(jnp.bfloat16)
    d_hidden = lax.dot_general(
        grad_out, w_out, (((1,), (1,)), ((), ())), preferred_element_type=jnp.float32
    ).astype(jnp.bfloat16)
    wout_term = lax.dot_general(
        hidden, grad_out, (((0,), (0,)), ((), ())), preferred_element_type=jnp.float32
    )
    d_monarch = (d_hidden.astype(jnp.float32) * gate.astype(jnp.float32)).astype(jnp.bfloat16)
    d_gate = (d_hidden.astype(jnp.float32) * current.astype(jnp.float32)).astype(jnp.bfloat16)
    grad_now = d_monarch
    for segment_bit in range(segment_total - 1, -1, -1):
        grad_partner = swapped(grad_now, "seq", segment_bit)
        upper_half = position >> segment_bit & 1
        own_coef = jnp.where(upper_half == 0, twiddle_w[segment_bit, 0], twiddle_w[segment_bit, 1])
        peer_coef = jnp.where(upper_half == 0, twiddle_w[segment_bit, 1], twiddle_w[segment_bit, 0])
        saved_own, saved_peer = stored[segment_bit]
        grad_float = grad_now.astype(jnp.float32)
        own_row = jnp.stack(
            [
                jnp.sum(grad_float * saved_own.astype(jnp.float32), axis=0),
                jnp.sum(grad_float * saved_peer.astype(jnp.float32), axis=0),
            ]
        )
        empty_row = jnp.zeros_like(own_row)
        partials[segment_bit] = jnp.where(
            upper_half == 0, jnp.stack([own_row, empty_row]), jnp.stack([empty_row, own_row])
        )
        grad_now = (
            own_coef[0] * grad_float + peer_coef[1] * grad_partner.astype(jnp.float32)
        ).astype(jnp.bfloat16)
    twiddle_grad = lax.psum(jnp.stack(partials), "seq")
    d_value = lax.dot_general(
        square_mix, grad_now, (((0,), (0,)), ((), ())), preferred_element_type=jnp.float32
    ).astype(jnp.bfloat16)
    grad_square = lax.dot_general(
        grad_now, value, (((1,), (1,)), ((), ())), preferred_element_type=jnp.float32
    )
    d_projected = jnp.concatenate([d_value, d_gate], axis=1)
    win_term = lax.dot_general(
        inputs, d_projected, (((0,), (0,)), ((), ())), preferred_element_type=jnp.float32
    )
    win_share, wout_share = (
        lax.psum_scatter(win_term, "seq", scatter_dimension=0, tiled=True),
        lax.psum_scatter(wout_term, "seq", scatter_dimension=0, tiled=True),
    )
    input_grad = lax.dot_general(
        d_projected, w_in, (((1,), (1,)), ((), ())), preferred_element_type=jnp.float32
    ).astype(jnp.bfloat16)
    handed = from_behind(input_grad, "pipe", -1)
    return (
        mixed_out[None],
        handed[None],
        win_share[None],
        wout_share[None],
        grad_square[None],
        twiddle_grad[None],
    )


def solution(mesh):
    in_specs = (
        P("pipe", "seq", None),
        P("pipe", "seq", None),
        P("pipe", None, None),
        P("pipe", None, None),
        P("pipe", "seq", None),
        P("pipe", None, None, None, None),
    )
    out_specs = (
        P("pipe", "seq", None),
        P("pipe", "seq", None),
        P("pipe", "seq", None),
        P("pipe", "seq", None),
        P("pipe", "seq", None),
        P("pipe", None, None, None, None),
    )
    return jax.shard_map(
        on_device, mesh=mesh, in_specs=in_specs, out_specs=out_specs, check_vma=False
    )
```

profile of v0, /device:TPU:2, one launch (start us, length us, event | category | flops | bytes accessed | tf_op | source)
XLA Modules:
  0.0 690.7 jit_solution(15321098489667302605)
XLA Ops:
  7.2 3.7 fusion.4
  12.5 1.8 collective-permute-done
  14.5 2.0 collective-permute-start.1
  16.5 12.2 %collective-permute-done.1 = bf16[256,1024]{1,0:T(8,128)(2,1)S(1)} collective-permute-done((bf16[256,1024]{1,0:T(8,128)(2,1)S(1)}, bf16[256,1024]{1,0:T(8,128)(2,1)S(1)}, u32[]{:S(2)}, u32[]{:S(2)}) %collective-permute-start.1) | collective-permute-done | bytes 524320 | tf_op jit(solution)/shard_map/ppermute | solution.py:14
  28.9 3.4 collective-permute-start.2
  32.3 22.8 %collective-permute-done.2 = bf16[256,1024]{1,0:T(8,128)(2,1)S(1)} collective-permute-done((bf16[256,1024]{1,0:T(8,128)(2,1)S(1)}, bf16[256,1024]{1,0:T(8,128)(2,1)S(1)}, u32[]{:S(2)}, u32[]{:S(2)}) %collective-permute-start.2) | collective-permute-done | bytes 524320 | tf_op jit(solution)/shard_map/ppermute | solution.py:14
  55.3 6.3 collective-permute-start.3
  61.6 23.0 %collective-permute-done.3 = bf16[256,1024]{1,0:T(8,128)(2,1)S(1)} collective-permute-done((bf16[256,1024]{1,0:T(8,128)(2,1)S(1)}, bf16[256,1024]{1,0:T(8,128)(2,1)S(1)}, u32[]{:S(2)}, u32[]{:S(2)}) %collective-permute-start.3) | collective-permute-done | bytes 524320 | tf_op jit(solution)/shard_map/ppermute | solution.py:14
  84.8 1.7 collective-permute-start.4
  86.5 11.2 %collective-permute-done.4 = bf16[256,1024]{1,0:T(8,128)(2,1)S(1)} collective-permute-done((bf16[256,1024]{1,0:T(8,128)(2,1)S(1)}, bf16[256,1024]{1,0:T(8,128)(2,1)S(1)}, u32[]{:S(2)}, u32[]{:S(2)}) %collective-permute-start.4) | collective-permute-done | bytes 524320 | tf_op jit(solution)/shard_map/ppermute | solution.py:14
  97.9 3.3 collective-permute-start.5
  101.9 9.5 %collective-permute-done.5 = bf16[256,1024]{1,0:T(8,128)(2,1)S(1)} collective-permute-done((bf16[256,1024]{1,0:T(8,128)(2,1)S(1)}, bf16[256,1024]{1,0:T(8,128)(2,1)S(1)}, u32[]{:S(2)}, u32[]{:S(2)}) %collective-permute-start.5) | collective-permute-done | bytes 524320 | tf_op jit(solution)/shard_map/ppermute | solution.py:14
  112.8 3.2 collective-permute-start.6
  116.0 9.3 %collective-permute-done.6 = bf16[256,1024]{1,0:T(8,128)(2,1)S(1)} collective-permute-done((bf16[256,1024]{1,0:T(8,128)(2,1)S(1)}, bf16[256,1024]{1,0:T(8,128)(2,1)S(1)}, u32[]{:S(2)}, u32[]{:S(2)}) %collective-permute-start.6) | collective-permute-done | bytes 524320 | tf_op jit(solution)/shard_map/ppermute | solution.py:14
  125.8 1.7 collective-permute-start.7
  127.4 9.4 %collective-permute-done.7 = bf16[256,1024]{1,0:T(8,128)(2,1)S(1)} collective-permute-done((bf16[256,1024]{1,0:T(8,128)(2,1)S(1)}, bf16[256,1024]{1,0:T(8,128)(2,1)S(1)}, u32[]{:S(2)}, u32[]{:S(2)}) %collective-permute-start.7) | collective-permute-done | bytes 524320 | tf_op jit(solution)/shard_map/ppermute | solution.py:14
  137.3 2.0 collective-permute-start.8
  139.3 19.1 %collective-permute-done.8 = bf16[256,1024]{1,0:T(8,128)(2,1)S(1)} collective-permute-done((bf16[256,1024]{1,0:T(8,128)(2,1)S(1)}, bf16[256,1024]{1,0:T(8,128)(2,1)S(1)}, u32[]{:S(2)}, u32[]{:S(2)}) %collective-permute-start.8) | collective-permute-done | bytes 524320 | tf_op jit(solution)/shard_map/ppermute | solution.py:14
  159.0 18.6 %collective-permute-done.9 = bf16[256,1024]{1,0:T(8,128)(2,1)S(1)} collective-permute-done((bf16[256,1024]{1,0:T(8,128)(2,1)S(1)}, bf16[256,1024]{1,0:T(8,128)(2,1)S(1)}, u32[]{:S(2)}, u32[]{:S(2)}) %collective-permute-start.9) | collective-permute-done | bytes 524320 | tf_op jit(solution)/shard_map/ppermute | solution.py:14
  178.1 1.6 collective-permute-start.10
  179.7 12.5 %collective-permute-done.10 = bf16[256,1024]{1,0:T(8,128)(2,1)S(1)} collective-permute-done((bf16[256,1024]{1,0:T(8,128)(2,1)S(1)}, bf16[256,1024]{1,0:T(8,128)(2,1)S(1)}, u32[]{:S(2)}, u32[]{:S(2)}) %collective-permute-start.10) | collective-permute-done | bytes 524320 | tf_op jit(solution)/shard_map/ppermute | solution.py:14
  192.8 1.9 collective-permute-done.11
  195.1 4.5 convolution_bitcast_fusion
  199.6 9.2 %copy.17 = f32[1024,2048]{1,0:T(8,128)} copy(f32[1024,2048]{0,1:T(8,128)} %convolution_bitcast_fusion) | data formatting | bytes 16777216
  210.0 3.9 fusion.64
  214.0 3.8 fusion.17
  217.9 2.6 collective-permute-start.12
  223.1 10.9 %collective-permute-done.12 = bf16[256,1024]{1,0:T(8,128)(2,1)} collective-permute-done((bf16[256,1024]{1,0:T(8,128)(2,1)S(1)}, bf16[256,1024]{1,0:T(8,128)(2,1)}, u32[]{:S(2)}, u32[]{:S(2)}) %collective-permute-start.12) | collective-permute-done | bytes 524320 | tf_op jit(solution)/shard_map/ppermute | solution.py:20
  234.0 126.0 %reduce-scatter.7.cloned.1.call-done = f32[16,2048]{1,0:T(8,128)} async-done(((f32[1024,2048]{1,0:T(8,128)}), f32[16,2048]{1,0:T(8,128)}) %reduce-scatter.7.cloned.1.call-update) | async-done | bytes 131088
  362.2 172.9 %all-reduce.14.cloned.1.call-done = f32[1,6,2,2,1024]{4,3,2,1,0:T(2,128)} async-done(((f32[1,6,2,2,1024]{4,3,2,1,0:T(2,128)}), f32[1,6,2,2,1024]{4,3,2,1,0:T(2,128)}) %all-reduce.14.cloned.1.call-update) | async-done | bytes 98320 | tf_op jit(solution)/shard_map/psum | solution.py:85
  535.0 145.7 %reduce-scatter.5.cloned.1.call-done = f32[16,1024]{1,0:T(8,128)} async-done(((f32[1024,1024]{1,0:T(8,128)}), f32[16,1024]{1,0:T(8,128)}) %reduce-scatter.5.cloned.1.call-update) | async-done | bytes 65552 | tf_op jit(solution)/shard_map/reduce_scatter | solution.py:98
  680.8 1.9 copy.26
  (83 shorter events, 15.0 us)
Async XLA Ops:
  7.2 94.0 %copy-start = (bf16[1,1024,1024]{2,1,0:T(8,128)(2,1)S(1)}, bf16[1,1024,1024]{2,1,0:T(8,128)(2,1)}, u32[]{:S(2)}) copy-start(bf16[1,1024,1024]{2,1,0:T(8,128)(2,1)} %param.9) | copy-start | bytes 6291460
  7.2 4.8 copy-start.13
  7.2 5.2 copy-start.11
  7.2 352.8 %reduce-scatter.7.cloned.1.call-start = ((), (), s32[]{:S(2)}) async-start(), calls=%async_computation.4 | async-start | bytes 8519680
  11.0 1.0 copy-start.1
  12.3 2.0 collective-permute-start
  14.5 14.2 %collective-permute-start.1 = (bf16[256,1024]{1,0:T(8,128)(2,1)S(1)}, bf16[256,1024]{1,0:T(8,128)(2,1)S(1)}, u32[]{:S(2)}, u32[]{:S(2)}) collective-permute-start(bf16[256,1024]{1,0:T(8,128)(2,1)S(1)} %fusion.26), channel_id=1, source_target_pairs={{0,2},{2,0},{1,3},{3,1},{4,6},{6,4},{5,7},{7,5},{8,10},{10,8},{9,1... | collective-permute-start | bytes 1572872 | tf_op jit(solution)/shard_map/ppermute | solution.py:14
  28.9 26.1 %collective-permute-start.2 = (bf16[256,1024]{1,0:T(8,128)(2,1)S(1)}, bf16[256,1024]{1,0:T(8,128)(2,1)S(1)}, u32[]{:S(2)}, u32[]{:S(2)}) collective-permute-start(bf16[256,1024]{1,0:T(8,128)(2,1)S(1)} %fusion.28), channel_id=1, source_target_pairs={{0,4},{4,0},{1,5},{5,1},{2,6},{6,2},{3,7},{7,3},{8,12},{12,8},{9,1... | collective-permute-start | bytes 1572872 | tf_op jit(solution)/shard_map/ppermute | solution.py:14
  55.1 46.1 %copy-start.10 = (bf16[1,256,1024]{2,1,0:T(8,128)(2,1)S(1)}, bf16[1,256,1024]{2,1,0:T(8,128)(2,1)}, u32[]{:S(2)}) copy-start(bf16[1,256,1024]{2,1,0:T(8,128)(2,1)} %param.7) | copy-start | bytes 1572868
  55.3 29.3 %collective-permute-start.3 = (bf16[256,1024]{1,0:T(8,128)(2,1)S(1)}, bf16[256,1024]{1,0:T(8,128)(2,1)S(1)}, u32[]{:S(2)}, u32[]{:S(2)}) collective-permute-start(bf16[256,1024]{1,0:T(8,128)(2,1)S(1)} %fusion.30), channel_id=1, source_target_pairs={{0,8},{8,0},{1,9},{9,1},{2,10},{10,2},{3,11},{11,3},{4,12},{12,4},... | collective-permute-start | bytes 1572872 | tf_op jit(solution)/shard_map/ppermute | solution.py:14
  84.8 12.8 %collective-permute-start.4 = (bf16[256,1024]{1,0:T(8,128)(2,1)S(1)}, bf16[256,1024]{1,0:T(8,128)(2,1)S(1)}, u32[]{:S(2)}, u32[]{:S(2)}) collective-permute-start(bf16[256,1024]{1,0:T(8,128)(2,1)S(1)} %fusion.32), channel_id=1, source_target_pairs={{0,16},{16,0},{1,17},{17,1},{2,18},{18,2},{3,19},{19,3},{4,20},{20... | collective-permute-start | bytes 1572872 | tf_op jit(solution)/shard_map/ppermute | solution.py:14
  97.9 13.5 %copy-start.2 = (bf16[256,2048]{1,0:T(8,128)(2,1)S(1)}, bf16[256,2048]{1,0:T(8,128)(2,1)}, u32[]{:S(2)}) copy-start(bf16[256,2048]{1,0:T(8,128)(2,1)} %copy-done.1) | copy-start | bytes 3145732
  97.9 13.5 %collective-permute-start.5 = (bf16[256,1024]{1,0:T(8,128)(2,1)S(1)}, bf16[256,1024]{1,0:T(8,128)(2,1)S(1)}, u32[]{:S(2)}, u32[]{:S(2)}) collective-permute-start(bf16[256,1024]{1,0:T(8,128)(2,1)S(1)} %fusion.34), channel_id=1, source_target_pairs={{0,32},{32,0},{1,33},{33,1},{2,34},{34,2},{3,35},{35,3},{4,36},{36... | collective-permute-start | bytes 1572872 | tf_op jit(solution)/shard_map/ppermute | solution.py:14
  112.8 82.3 %copy-start.4 = (bf16[256,1024]{1,0:T(8,128)(2,1)}, bf16[256,1024]{1,0:T(8,128)(2,1)S(1)}, u32[]{:S(2)}) copy-start(bf16[256,1024]{1,0:T(8,128)(2,1)S(1)} %get-tuple-element.38) | copy-start | bytes 1572868
  112.8 12.6 %collective-permute-start.6 = (bf16[256,1024]{1,0:T(8,128)(2,1)S(1)}, bf16[256,1024]{1,0:T(8,128)(2,1)S(1)}, u32[]{:S(2)}, u32[]{:S(2)}) collective-permute-start(bf16[256,1024]{1,0:T(8,128)(2,1)S(1)} %get-tuple-element.30), channel_id=1, source_target_pairs={{0,32},{32,0},{1,33},{33,1},{2,34},{34,2},{3,35},{35,3},{4,36},{36... | collective-permute-start | bytes 1572872 | tf_op jit(solution)/shard_map/ppermute | solution.py:14
  125.8 11.1 %collective-permute-start.7 = (bf16[256,1024]{1,0:T(8,128)(2,1)S(1)}, bf16[256,1024]{1,0:T(8,128)(2,1)S(1)}, u32[]{:S(2)}, u32[]{:S(2)}) collective-permute-start(bf16[256,1024]{1,0:T(8,128)(2,1)S(1)} %get-tuple-element.31), channel_id=1, source_target_pairs={{0,16},{16,0},{1,17},{17,1},{2,18},{18,2},{3,19},{19,3},{4,20},{20... | collective-permute-start | bytes 1572872 | tf_op jit(solution)/shard_map/ppermute | solution.py:14
  137.3 21.1 %collective-permute-start.8 = (bf16[256,1024]{1,0:T(8,128)(2,1)S(1)}, bf16[256,1024]{1,0:T(8,128)(2,1)S(1)}, u32[]{:S(2)}, u32[]{:S(2)}) collective-permute-start(bf16[256,1024]{1,0:T(8,128)(2,1)S(1)} %get-tuple-element.32), channel_id=1, source_target_pairs={{0,8},{8,0},{1,9},{9,1},{2,10},{10,2},{3,11},{11,3},{4,12},{12,4},... | collective-permute-start | bytes 1572872 | tf_op jit(solution)/shard_map/ppermute | solution.py:14
  158.9 18.7 %collective-permute-start.9 = (bf16[256,1024]{1,0:T(8,128)(2,1)S(1)}, bf16[256,1024]{1,0:T(8,128)(2,1)S(1)}, u32[]{:S(2)}, u32[]{:S(2)}) collective-permute-start(bf16[256,1024]{1,0:T(8,128)(2,1)S(1)} %get-tuple-element.33), channel_id=1, source_target_pairs={{0,4},{4,0},{1,5},{5,1},{2,6},{6,2},{3,7},{7,3},{8,12},{12,8},{9,1... | collective-permute-start | bytes 1572872 | tf_op jit(solution)/shard_map/ppermute | solution.py:14
  178.1 14.1 %collective-permute-start.10 = (bf16[256,1024]{1,0:T(8,128)(2,1)S(1)}, bf16[256,1024]{1,0:T(8,128)(2,1)S(1)}, u32[]{:S(2)}, u32[]{:S(2)}) collective-permute-start(bf16[256,1024]{1,0:T(8,128)(2,1)S(1)} %get-tuple-element.34), channel_id=1, source_target_pairs={{0,2},{2,0},{1,3},{3,1},{4,6},{6,4},{5,7},{7,5},{8,10},{10,8},{9,1... | collective-permute-start | bytes 1572872 | tf_op jit(solution)/shard_map/ppermute | solution.py:14
  192.2 2.9 copy-start.6
  192.6 2.0 copy-start.7
  192.6 2.0 collective-permute-start.11
  194.6 5.0 copy-start.14
  195.1 4.5 copy-start.9
  208.8 1.2 copy-start.3
  208.8 326.2 %all-reduce.14.cloned.1.call-start = ((), (), s32[]{:S(2)}) async-start(), calls=%async_computation.3 | async-start | bytes 196608 | tf_op jit(solution)/shard_map/psum | solution.py:85
  209.1 0.6 copy-start.12
  209.8 470.9 %reduce-scatter.5.cloned.1.call-start = ((), (), s32[]{:S(2)}) async-start(), calls=%async_computation.2 | async-start | bytes 4259840 | tf_op jit(solution)/shard_map/reduce_scatter | solution.py:98
  214.0 6.5 copy-start.5
  217.9 4.1 copy-start.8
  217.9 4.1 copy-start.15
  217.9 16.1 %collective-permute-start.12 = (bf16[256,1024]{1,0:T(8,128)(2,1)S(1)}, bf16[256,1024]{1,0:T(8,128)(2,1)}, u32[]{:S(2)}, u32[]{:S(2)}) collective-permute-start(bf16[256,1024]{1,0:T(8,128)(2,1)S(1)} %fusion.17), channel_id=1, source_target_pairs={{64,0},{128,64},{192,128},{65,1},{129,65},{193,129},{66,2},{130,66... | collective-permute-start | bytes 1572872 | tf_op jit(solution)/shard_map/ppermute | solution.py:20
Sparse Core Ops, SparseCore 0:
  209.0 150.9 reduce-scatter.6
  364.0 170.9 all-reduce.13
  539.8 140.9 reduce-scatter.4
where the time goes:
time: 691 us
  waiting for transfers between devices  607 us (88%)
  starting transfers between devices  28 us (4%)
  matrix products  20.1 us (3%)
  local copies, waits for them, and re-layouts  16.7 us (2%)
  between operations  14.1 us (2%)
    psum x1, waiting for transfers between devices, on_device(): twiddle_grad = lax.psum(jnp.stack(partials), 'seq')  173 us
    ppermute x12, waiting for transfers between devices, swapped(): return lax.ppermute(block, axis, route)  151 us
    reduce_scatter x1, waiting for transfers between devices, on_device(): lax.psum_scatter(wout_term, 'seq', scatter_dimension=0, tiled=True)  146 us
    unnamed x4, waiting for transfers between devices  126 us
    ppermute x12, starting transfers between devices, swapped(): return lax.ppermute(block, axis, route)  25.3 us
    unnamed x37, local copies, waits for them, and re-layouts  16.7 us
  transfers between devices with their start and end apart: 16, of which 16 were waited for; matrix products, arithmetic and copies ran while one was open for 2% of the time, Pallas kernels for 0%

commit v1 on v0

--- a/solution.py
+++ b/solution.py
@@ -82,7 +82,7 @@
         grad_now = (
             own_coef[0] * grad_float + peer_coef[1] * grad_partner.astype(jnp.float32)
         ).astype(jnp.bfloat16)
-    twiddle_grad = lax.psum(jnp.stack(partials), "seq")
+    twiddle_grad = jnp.sum(lax.all_gather(jnp.stack(partials), "seq"), axis=0)
     d_value = lax.dot_general(
         square_mix, grad_now, (((0,), (0,)), ((), ())), preferred_element_type=jnp.float32
     ).astype(jnp.bfloat16)

time: 691 us -> 583 us (0.84)
  waiting for transfers between devices: 607 us -> 490 us
  other arithmetic: 4.89 us -> 12.4 us
    psum x1 -> x0, waiting for transfers between devices: 173 us -> none  [on_device(): twiddle_grad = lax.psum(jnp.stack(partials), 'seq')]
    all_gather x0 -> x1, waiting for transfers between devices: none -> 35.6 us  [on_device(): twiddle_grad = jnp.sum(lax.all_gather(jnp.stack(partials), 'seq'), axis=0)]
    unnamed x4, waiting for transfers between devices: 126 us -> 147 us
    unnamed x37 -> x34, local copies, waits for them, and re-layouts: 16.7 us -> 16.9 us
  transfers between devices with their start and end apart: 16 -> 16, of which waited for: 16 -> 16; matrix products, arithmetic and copies ran while one was open for 2% -> 6% of each run, Pallas kernels for 0% -> 0%
where the time goes in v1:
time: 583 us
  waiting for transfers between devices  490 us (84%)
  starting transfers between devices  28 us (5%)
  matrix products  21.3 us (4%)
  local copies, waits for them, and re-layouts  16.9 us (3%)
  between operations  14.1 us (2%)
  other arithmetic  12.4 us (2%)
    ppermute x12, waiting for transfers between devices, swapped(): return lax.ppermute(block, axis, route)  151 us
    unnamed x4, waiting for transfers between devices  147 us
    reduce_scatter x1, waiting for transfers between devices, on_device(): lax.psum_scatter(wout_term, 'seq', scatter_dimension=0, tiled=True)  145 us
    all_gather x1, waiting for transfers between devices, on_device(): twiddle_grad = jnp.sum(lax.all_gather(jnp.stack(partials), 'seq'), axis=0)  35.6 us
    ppermute x12, starting transfers between devices, swapped(): return lax.ppermute(block, axis, route)  25.3 us
    unnamed x34, local copies, waits for them, and re-layouts  16.9 us
  transfers between devices with their start and end apart: 16, of which 16 were waited for; matrix products, arithmetic and copies ran while one was open for 6% of the time, Pallas kernels for 0%

profile of v1, /device:TPU:2, one launch (start us, length us, event | category | flops | bytes accessed | tf_op | source)
XLA Modules:
  0.0 582.7 jit_solution(9527424359201713282)
XLA Ops:
  7.2 3.7 fusion.4
  12.5 1.8 collective-permute-done
  14.5 2.0 collective-permute-start.1
  16.5 12.2 %collective-permute-done.1 = bf16[256,1024]{1,0:T(8,128)(2,1)S(1)} collective-permute-done((bf16[256,1024]{1,0:T(8,128)(2,1)S(1)}, bf16[256,1024]{1,0:T(8,128)(2,1)S(1)}, u32[]{:S(2)}, u32[]{:S(2)}) %collective-permute-start.1) | collective-permute-done | bytes 524320 | tf_op jit(solution)/shard_map/ppermute | solution.py:14
  29.0 3.4 collective-permute-start.2
  32.3 22.8 %collective-permute-done.2 = bf16[256,1024]{1,0:T(8,128)(2,1)S(1)} collective-permute-done((bf16[256,1024]{1,0:T(8,128)(2,1)S(1)}, bf16[256,1024]{1,0:T(8,128)(2,1)S(1)}, u32[]{:S(2)}, u32[]{:S(2)}) %collective-permute-start.2) | collective-permute-done | bytes 524320 | tf_op jit(solution)/shard_map/ppermute | solution.py:14
  55.3 6.3 %collective-permute-start.3 = (bf16[256,1024]{1,0:T(8,128)(2,1)S(1)}, bf16[256,1024]{1,0:T(8,128)(2,1)S(1)}, u32[]{:S(2)}, u32[]{:S(2)}) collective-permute-start(bf16[256,1024]{1,0:T(8,128)(2,1)S(1)} %fusion.30), channel_id=1, source_target_pairs={{0,8},{8,0},{1,9},{9,1},{2,10},{10,2},{3,11},{11,3},{4,12},{12,4},... | collective-permute-start | bytes 1572872 | tf_op jit(solution)/shard_map/ppermute | solution.py:14
  61.6 23.0 %collective-permute-done.3 = bf16[256,1024]{1,0:T(8,128)(2,1)S(1)} collective-permute-done((bf16[256,1024]{1,0:T(8,128)(2,1)S(1)}, bf16[256,1024]{1,0:T(8,128)(2,1)S(1)}, u32[]{:S(2)}, u32[]{:S(2)}) %collective-permute-start.3) | collective-permute-done | bytes 524320 | tf_op jit(solution)/shard_map/ppermute | solution.py:14
  84.9 1.7 collective-permute-start.4
  86.5 11.2 %collective-permute-done.4 = bf16[256,1024]{1,0:T(8,128)(2,1)S(1)} collective-permute-done((bf16[256,1024]{1,0:T(8,128)(2,1)S(1)}, bf16[256,1024]{1,0:T(8,128)(2,1)S(1)}, u32[]{:S(2)}, u32[]{:S(2)}) %collective-permute-start.4) | collective-permute-done | bytes 524320 | tf_op jit(solution)/shard_map/ppermute | solution.py:14
  97.9 3.3 collective-permute-start.5
  102.0 9.5 %collective-permute-done.5 = bf16[256,1024]{1,0:T(8,128)(2,1)S(1)} collective-permute-done((bf16[256,1024]{1,0:T(8,128)(2,1)S(1)}, bf16[256,1024]{1,0:T(8,128)(2,1)S(1)}, u32[]{:S(2)}, u32[]{:S(2)}) %collective-permute-start.5) | collective-permute-done | bytes 524320 | tf_op jit(solution)/shard_map/ppermute | solution.py:14
  112.9 3.2 collective-permute-start.6
  116.2 9.3 %collective-permute-done.6 = bf16[256,1024]{1,0:T(8,128)(2,1)S(1)} collective-permute-done((bf16[256,1024]{1,0:T(8,128)(2,1)S(1)}, bf16[256,1024]{1,0:T(8,128)(2,1)S(1)}, u32[]{:S(2)}, u32[]{:S(2)}) %collective-permute-start.6) | collective-permute-done | bytes 524320 | tf_op jit(solution)/shard_map/ppermute | solution.py:14
  125.9 1.7 collective-permute-start.7
  127.6 9.5 %collective-permute-done.7 = bf16[256,1024]{1,0:T(8,128)(2,1)S(1)} collective-permute-done((bf16[256,1024]{1,0:T(8,128)(2,1)S(1)}, bf16[256,1024]{1,0:T(8,128)(2,1)S(1)}, u32[]{:S(2)}, u32[]{:S(2)}) %collective-permute-start.7) | collective-permute-done | bytes 524320 | tf_op jit(solution)/shard_map/ppermute | solution.py:14
  137.5 2.0 collective-permute-start.8
  139.5 19.1 %collective-permute-done.8 = bf16[256,1024]{1,0:T(8,128)(2,1)S(1)} collective-permute-done((bf16[256,1024]{1,0:T(8,128)(2,1)S(1)}, bf16[256,1024]{1,0:T(8,128)(2,1)S(1)}, u32[]{:S(2)}, u32[]{:S(2)}) %collective-permute-start.8) | collective-permute-done | bytes 524320 | tf_op jit(solution)/shard_map/ppermute | solution.py:14
  159.2 18.6 %collective-permute-done.9 = bf16[256,1024]{1,0:T(8,128)(2,1)S(1)} collective-permute-done((bf16[256,1024]{1,0:T(8,128)(2,1)S(1)}, bf16[256,1024]{1,0:T(8,128)(2,1)S(1)}, u32[]{:S(2)}, u32[]{:S(2)}) %collective-permute-start.9) | collective-permute-done | bytes 524320 | tf_op jit(solution)/shard_map/ppermute | solution.py:14
  180.0 12.4 %collective-permute-done.10 = bf16[256,1024]{1,0:T(8,128)(2,1)S(1)} collective-permute-done((bf16[256,1024]{1,0:T(8,128)(2,1)S(1)}, bf16[256,1024]{1,0:T(8,128)(2,1)S(1)}, u32[]{:S(2)}, u32[]{:S(2)}) %collective-permute-start.10) | collective-permute-done | bytes 524320 | tf_op jit(solution)/shard_map/ppermute | solution.py:14
  194.5 2.1 collective-permute-done.11
  199.1 4.5 convolution_bitcast_fusion
  203.6 9.2 %copy.17 = f32[1024,2048]{1,0:T(8,128)} copy(f32[1024,2048]{0,1:T(8,128)} %convolution_bitcast_fusion) | data formatting | bytes 16777216
  214.0 3.9 fusion.64
  218.0 3.9 fusion.17
  221.9 2.6 collective-permute-start.12
  227.1 10.9 %collective-permute-done.12 = bf16[256,1024]{1,0:T(8,128)(2,1)} collective-permute-done((bf16[256,1024]{1,0:T(8,128)(2,1)S(1)}, bf16[256,1024]{1,0:T(8,128)(2,1)}, u32[]{:S(2)}, u32[]{:S(2)}) %collective-permute-start.12) | collective-permute-done | bytes 524320 | tf_op jit(solution)/shard_map/ppermute | solution.py:20
  238.0 35.6 %all-gather.3.cloned.1.call-done = f32[384,2,2,1024]{3,2,1,0:T(2,128)} async-done(((f32[6,2,2,1024]{3,2,1,0:T(2,128)}), f32[384,2,2,1024]{3,2,1,0:T(2,128)}) %all-gather.3.cloned.1.call-update) | async-done | bytes 6291472 | tf_op jit(solution)/shard_map/all_gather | solution.py:85
  273.6 6.6 %reduce_sum.129 = f32[6,2,2,1024]{3,2,1,0:T(2,128)} reduce(f32[64,6,2,2,1024]{4,3,2,1,0:T(2,128)} %bitcast.106, f32[]{:T(128)} %constant.6.clone.1), dimensions={0}, to_apply=%region_14.15 | reduce | flops 1548288 | bytes 6389764 | tf_op jit(solution)/shard_map/reduce_sum | solution.py:85
  280.1 146.8 %reduce-scatter.7.cloned.1.call-done = f32[16,2048]{1,0:T(8,128)} async-done(((f32[1024,2048]{1,0:T(8,128)}), f32[16,2048]{1,0:T(8,128)}) %reduce-scatter.7.cloned.1.call-update) | async-done | bytes 131088
  429.1 145.2 %reduce-scatter.5.cloned.1.call-done = f32[16,1024]{1,0:T(8,128)} async-done(((f32[1024,1024]{1,0:T(8,128)}), f32[16,1024]{1,0:T(8,128)}) %reduce-scatter.5.cloned.1.call-update) | async-done | bytes 65552 | tf_op jit(solution)/shard_map/reduce_scatter | solution.py:98
  574.3 1.9 copy.25
  (81 shorter events, 19.0 us)
Async XLA Ops:
  7.2 94.0 %copy-start = (bf16[1,1024,1024]{2,1,0:T(8,128)(2,1)S(1)}, bf16[1,1024,1024]{2,1,0:T(8,128)(2,1)}, u32[]{:S(2)}) copy-start(bf16[1,1024,1024]{2,1,0:T(8,128)(2,1)} %param.9) | copy-start | bytes 6291460
  7.2 4.8 copy-start.12
  7.2 5.2 copy-start.10
  7.2 266.4 %all-gather.3.cloned.1.call-start = ((), (), s32[]{:S(2)}) async-start(), calls=%async_computation.3 | async-start | bytes 6389760 | tf_op jit(solution)/shard_map/all_gather | solution.py:85
  11.0 1.0 copy-start.1
  12.3 2.0 collective-permute-start
  14.5 14.2 %collective-permute-start.1 = (bf16[256,1024]{1,0:T(8,128)(2,1)S(1)}, bf16[256,1024]{1,0:T(8,128)(2,1)S(1)}, u32[]{:S(2)}, u32[]{:S(2)}) collective-permute-start(bf16[256,1024]{1,0:T(8,128)(2,1)S(1)} %fusion.26), channel_id=1, source_target_pairs={{0,2},{2,0},{1,3},{3,1},{4,6},{6,4},{5,7},{7,5},{8,10},{10,8},{9,1... | collective-permute-start | bytes 1572872 | tf_op jit(solution)/shard_map/ppermute | solution.py:14
  29.0 26.1 %collective-permute-start.2 = (bf16[256,1024]{1,0:T(8,128)(2,1)S(1)}, bf16[256,1024]{1,0:T(8,128)(2,1)S(1)}, u32[]{:S(2)}, u32[]{:S(2)}) collective-permute-start(bf16[256,1024]{1,0:T(8,128)(2,1)S(1)} %fusion.28), channel_id=1, source_target_pairs={{0,4},{4,0},{1,5},{5,1},{2,6},{6,2},{3,7},{7,3},{8,12},{12,8},{9,1... | collective-permute-start | bytes 1572872 | tf_op jit(solution)/shard_map/ppermute | solution.py:14
  55.1 46.1 %copy-start.9 = (bf16[1,256,1024]{2,1,0:T(8,128)(2,1)S(1)}, bf16[1,256,1024]{2,1,0:T(8,128)(2,1)}, u32[]{:S(2)}) copy-start(bf16[1,256,1024]{2,1,0:T(8,128)(2,1)} %param.7) | copy-start | bytes 1572868
  55.3 29.3 %collective-permute-start.3 = (bf16[256,1024]{1,0:T(8,128)(2,1)S(1)}, bf16[256,1024]{1,0:T(8,128)(2,1)S(1)}, u32[]{:S(2)}, u32[]{:S(2)}) collective-permute-start(bf16[256,1024]{1,0:T(8,128)(2,1)S(1)} %fusion.30), channel_id=1, source_target_pairs={{0,8},{8,0},{1,9},{9,1},{2,10},{10,2},{3,11},{11,3},{4,12},{12,4},... | collective-permute-start | bytes 1572872 | tf_op jit(solution)/shard_map/ppermute | solution.py:14
  84.9 12.8 %collective-permute-start.4 = (bf16[256,1024]{1,0:T(8,128)(2,1)S(1)}, bf16[256,1024]{1,0:T(8,128)(2,1)S(1)}, u32[]{:S(2)}, u32[]{:S(2)}) collective-permute-start(bf16[256,1024]{1,0:T(8,128)(2,1)S(1)} %fusion.32), channel_id=1, source_target_pairs={{0,16},{16,0},{1,17},{17,1},{2,18},{18,2},{3,19},{19,3},{4,20},{20... | collective-permute-start | bytes 1572872 | tf_op jit(solution)/shard_map/ppermute | solution.py:14
  97.9 13.5 %copy-start.2 = (bf16[256,2048]{1,0:T(8,128)(2,1)S(1)}, bf16[256,2048]{1,0:T(8,128)(2,1)}, u32[]{:S(2)}) copy-start(bf16[256,2048]{1,0:T(8,128)(2,1)} %copy-done.1) | copy-start | bytes 3145732
  97.9 13.5 %collective-permute-start.5 = (bf16[256,1024]{1,0:T(8,128)(2,1)S(1)}, bf16[256,1024]{1,0:T(8,128)(2,1)S(1)}, u32[]{:S(2)}, u32[]{:S(2)}) collective-permute-start(bf16[256,1024]{1,0:T(8,128)(2,1)S(1)} %fusion.34), channel_id=1, source_target_pairs={{0,32},{32,0},{1,33},{33,1},{2,34},{34,2},{3,35},{35,3},{4,36},{36... | collective-permute-start | bytes 1572872 | tf_op jit(solution)/shard_map/ppermute | solution.py:14
  112.9 12.6 %collective-permute-start.6 = (bf16[256,1024]{1,0:T(8,128)(2,1)S(1)}, bf16[256,1024]{1,0:T(8,128)(2,1)S(1)}, u32[]{:S(2)}, u32[]{:S(2)}) collective-permute-start(bf16[256,1024]{1,0:T(8,128)(2,1)S(1)} %get-tuple-element.30), channel_id=1, source_target_pairs={{0,32},{32,0},{1,33},{33,1},{2,34},{34,2},{3,35},{35,3},{4,36},{36... | collective-permute-start | bytes 1572872 | tf_op jit(solution)/shard_map/ppermute | solution.py:14
  125.9 11.1 %collective-permute-start.7 = (bf16[256,1024]{1,0:T(8,128)(2,1)S(1)}, bf16[256,1024]{1,0:T(8,128)(2,1)S(1)}, u32[]{:S(2)}, u32[]{:S(2)}) collective-permute-start(bf16[256,1024]{1,0:T(8,128)(2,1)S(1)} %get-tuple-element.31), channel_id=1, source_target_pairs={{0,16},{16,0},{1,17},{17,1},{2,18},{18,2},{3,19},{19,3},{4,20},{20... | collective-permute-start | bytes 1572872 | tf_op jit(solution)/shard_map/ppermute | solution.py:14
  137.5 21.1 %collective-permute-start.8 = (bf16[256,1024]{1,0:T(8,128)(2,1)S(1)}, bf16[256,1024]{1,0:T(8,128)(2,1)S(1)}, u32[]{:S(2)}, u32[]{:S(2)}) collective-permute-start(bf16[256,1024]{1,0:T(8,128)(2,1)S(1)} %get-tuple-element.32), channel_id=1, source_target_pairs={{0,8},{8,0},{1,9},{9,1},{2,10},{10,2},{3,11},{11,3},{4,12},{12,4},... | collective-permute-start | bytes 1572872 | tf_op jit(solution)/shard_map/ppermute | solution.py:14
  159.0 18.8 %collective-permute-start.9 = (bf16[256,1024]{1,0:T(8,128)(2,1)S(1)}, bf16[256,1024]{1,0:T(8,128)(2,1)S(1)}, u32[]{:S(2)}, u32[]{:S(2)}) collective-permute-start(bf16[256,1024]{1,0:T(8,128)(2,1)S(1)} %get-tuple-element.33), channel_id=1, source_target_pairs={{0,4},{4,0},{1,5},{5,1},{2,6},{6,2},{3,7},{7,3},{8,12},{12,8},{9,1... | collective-permute-start | bytes 1572872 | tf_op jit(solution)/shard_map/ppermute | solution.py:14
  178.2 14.1 %collective-permute-start.10 = (bf16[256,1024]{1,0:T(8,128)(2,1)S(1)}, bf16[256,1024]{1,0:T(8,128)(2,1)S(1)}, u32[]{:S(2)}, u32[]{:S(2)}) collective-permute-start(bf16[256,1024]{1,0:T(8,128)(2,1)S(1)} %get-tuple-element.34), channel_id=1, source_target_pairs={{0,2},{2,0},{1,3},{3,1},{4,6},{6,4},{5,7},{7,5},{8,10},{10,8},{9,1... | collective-permute-start | bytes 1572872 | tf_op jit(solution)/shard_map/ppermute | solution.py:14
  193.6 5.5 copy-start.4
  193.6 5.5 copy-start.6
  193.7 0.6 copy-start.11
  194.4 232.6 %reduce-scatter.7.cloned.1.call-start = ((), (), s32[]{:S(2)}) async-start(), calls=%async_computation.4 | async-start | bytes 8519680
  194.4 2.2 collective-permute-start.11
  196.6 1.6 copy-start.13
  198.3 0.8 copy-start.8
  212.8 1.2 copy-start.3
  212.8 361.5 %reduce-scatter.5.cloned.1.call-start = ((), (), s32[]{:S(2)}) async-start(), calls=%async_computation.2 | async-start | bytes 4259840 | tf_op jit(solution)/shard_map/reduce_scatter | solution.py:98
  218.0 6.5 %copy-start.5 = (bf16[256,1024]{1,0:T(8,128)(2,1)S(1)}, bf16[256,1024]{1,0:T(8,128)(2,1)}, u32[]{:S(2)}) copy-start(bf16[256,1024]{1,0:T(8,128)(2,1)} %get-tuple-element.39) | copy-start | bytes 1572868
  221.9 4.1 copy-start.7
  221.9 4.1 copy-start.14
  221.9 16.1 %collective-permute-start.12 = (bf16[256,1024]{1,0:T(8,128)(2,1)S(1)}, bf16[256,1024]{1,0:T(8,128)(2,1)}, u32[]{:S(2)}, u32[]{:S(2)}) collective-permute-start(bf16[256,1024]{1,0:T(8,128)(2,1)S(1)} %fusion.17), channel_id=1, source_target_pairs={{64,0},{128,64},{192,128},{65,1},{129,65},{193,129},{66,2},{130,66... | collective-permute-start | bytes 1572872 | tf_op jit(solution)/shard_map/ppermute | solution.py:20
Sparse Core Ops, SparseCore 0:
  194.5 79.0 all-gather.2
  277.8 149.1 reduce-scatter.6
  431.6 142.6 reduce-scatter.4
